TPU v7x, 256 devices: a whole 4x4x8 slice. The times are simulated.
256 devices in a mesh: row: 16 (over z_hi, y), col: 16 (over z_lo, x, core).
Axes of the slice: x: 4, y: 4, z: 8 (z_hi: 4, z_lo: 2; z = z_hi * 2 + z_lo), core: 2. Of those that a mesh axis runs over, the one named last changes fastest.
Arguments:
- spectra: bfloat16 [4096, 128], P(('row', 'col')), may hold values from -6 to 6
- residual: bfloat16 [768, 128, 128, 128], P(('row', 'col')), may hold values from -1.5 to 1.5
- slot_tile: int32 [768], P(('row', 'col')), may hold values from -1 to 527, as said below
- tile_blocks: int32 [528, 2], replicated, may hold values from 0 to 31, as said below
Outputs:
- spectra_grad: float32 [4096, 128], P(('row', 'col'))
Inputs may be any that keep to these rules, and one draw needn't show every extreme that they name: `slot_tile`: every tile number appears in exactly one slot and all other slots hold -1. A tile with row block p and column block q sits on the device at mesh position (p mod 16, q mod 16), that is device number (p mod 16) * 16 + q mod 16 in the order of row+col. `tile_blocks`: row t holds the row block and the column block of tile t, the row block no larger than the column block; every such pair of blocks is exactly one tile.
All inputs are finite; a program needn't handle non-finite values.
Results may differ from a plain program's by a relative error of at most 0.004.
Values may be sent and summed in bfloat16 or wider, within the bound.
No kernel may reach another device: no remote copies, remote signals or barrier semaphores. Data moves between devices by JAX's collectives and lax.ppermute only.
A program may use at most 128 MiB of HBM per device.

v0:
```python
import math
import jax
import jax.numpy as jnp
from jax import lax
from jax.sharding import PartitionSpec as P


def dft_table(lag_count, freq_count):
    lag_index = jnp.arange(lag_count, dtype=jnp.int32) - lag_count // 2
    freq_index = jnp.arange(freq_count, dtype=jnp.int32)
    phase_steps = lag_index[:, None] * freq_index[None, :] % lag_count
    angles = phase_steps.astype(jnp.float32) * (2.0 * math.pi / lag_count)
    cosine = jnp.cos(angles) / lag_count
    sine = -jnp.sin(angles) / lag_count
    return jnp.concatenate([cosine, sine], axis=1).astype(jnp.bfloat16)


def pair_terms(spectral, row_spec, col_spec, freq_count):
    real_part = spectral[:, :, :freq_count]
    imag_part = spectral[:, :, freq_count:]
    row_re = row_spec[:, :freq_count].astype(jnp.float32)
    row_im = row_spec[:, freq_count:].astype(jnp.float32)
    col_re = col_spec[:, :freq_count].astype(jnp.float32)
    col_im = col_spec[:, freq_count:].astype(jnp.float32)
    row_gain_re = jnp.sum(real_part * col_re[None] - imag_part * col_im[None], axis=1)
    row_gain_im = jnp.sum(real_part * col_im[None] + imag_part * col_re[None], axis=1)
    col_gain_re = jnp.sum(real_part * row_re[:, None] + imag_part * row_im[:, None], axis=0)
    col_gain_im = jnp.sum(real_part * row_im[:, None] - imag_part * row_re[:, None], axis=0)
    row_gain = jnp.concatenate([row_gain_re, row_gain_im], axis=1)
    col_gain = jnp.concatenate([col_gain_re, col_gain_im], axis=1)
    return (row_gain, col_gain)


def block_major(flat, row_count, col_count, block_count, tile_size):
    per_row = block_count // row_count
    piece = tile_size // col_count
    grid = flat.reshape(row_count, col_count, per_row, piece, flat.shape[1])
    return jnp.transpose(grid, (2, 0, 1, 3, 4)).reshape(block_count, tile_size, flat.shape[1])


def station_major(blocks, row_count, col_count, block_count, tile_size):
    per_row = block_count // row_count
    piece = tile_size // col_count
    grid = blocks.reshape(per_row, row_count, col_count, piece, blocks.shape[2])
    return jnp.transpose(grid, (1, 2, 0, 3, 4)).reshape(block_count * tile_size, blocks.shape[2])


def add_block(gradient, contrib, index):
    current = lax.dynamic_index_in_dim(gradient, index, 0, keepdims=True)
    return lax.dynamic_update_index_in_dim(gradient, current + contrib[None], index, 0)


def on_device(spectra, residual, slot_tile, tile_blocks):
    slot_count, tile_size, _, lag_count = residual.shape
    freq_count = spectra.shape[1] // 2
    width = 2 * freq_count
    row_count = lax.axis_size("row")
    col_count = lax.axis_size("col")
    block_count = 2 * min(row_count, col_count)
    dft = dft_table(lag_count, freq_count)
    tile_total = tile_blocks.shape[0]
    matches = (slot_tile[:, None] == jnp.arange(tile_total, dtype=jnp.int32)[None, :]).astype(
        jnp.int32
    )
    chosen = jnp.sum(matches[:, :, None] * tile_blocks[None, :, :], axis=1)
    filled = slot_tile >= 0
    station_ids = jnp.arange(tile_size, dtype=jnp.int32)
    upper = station_ids[:, None] < station_ids[None, :]
    gathered = lax.all_gather(spectra, ("row", "col"), axis=0, tiled=True)
    row_source = block_major(gathered, row_count, col_count, block_count, tile_size)
    row_div = 1
    col_div = 1
    row_grad = jnp.zeros((row_source.shape[0], tile_size, width), jnp.float32)
    col_grad = jnp.zeros((row_source.shape[0], tile_size, width), jnp.float32)
    for slot_index in range(slot_count):
        row_block = chosen[slot_index, 0]
        col_block = chosen[slot_index, 1]
        pair_mask = (jnp.where(row_block == col_block, upper, True) & filled[slot_index]).astype(
            jnp.float32
        )
        tile_data = residual[slot_index]
        row_index = row_block // row_div
        col_index = col_block // col_div
        row_spec = lax.dynamic_index_in_dim(row_source, row_index, 0, keepdims=False)
        col_spec = lax.dynamic_index_in_dim(row_source, col_index, 0, keepdims=False)
        spectral = jnp.dot(
            tile_data.reshape(tile_size * tile_size, lag_count),
            dft,
            preferred_element_type=jnp.float32,
        )
        spectral = spectral.reshape(tile_size, tile_size, width) * pair_mask[:, :, None]
        row_gain, col_gain = pair_terms(spectral, row_spec, col_spec, freq_count)
        row_grad = add_block(row_grad, row_gain, row_index)
        col_grad = add_block(col_grad, col_gain, col_index)
    gradient = station_major(row_grad + col_grad, row_count, col_count, block_count, tile_size)
    return lax.psum_scatter(gradient, ("row", "col"), scatter_dimension=0, tiled=True)


def solution(mesh):
    return jax.shard_map(
        on_device,
        mesh=mesh,
        in_specs=(
            P(("row", "col"), None),
            P(("row", "col"), None, None, None),
            P(("row", "col")),
            P(),
        ),
        out_specs=P(("row", "col"), None),
        check_vma=False,
    )
```

profile of v0, /device:TPU:0, one launch (start us, length us, event | category | flops | bytes accessed | tf_op | source)
XLA Modules:
  0.0 1714.3 jit_solution(4478842264416761182)
XLA Ops:
  6.5 0.7 all-gather.2.cloned.1.call-update
  7.3 0.0 reduce-scatter.2.cloned.1.call-start
  7.3 0.7 fusion.25
  8.0 0.7 broadcast_compare_fusion
  8.7 0.8 multiply_reduce_fusion
  9.5 0.6 fusion.36
  10.1 0.7 fusion.37
  10.8 0.2 multiply_convert_fusion.1
  11.0 8.2 fusion.29
  19.1 4.5 convolution_bitcast_fusion.2
  23.6 4.5 convolution_bitcast_fusion.1
  28.1 4.5 convolution_bitcast_fusion
  33.7 0.6 fusion.14
  35.4 0.7 fusion.16
  44.6 8.2 copy.80
  52.9 8.2 copy.81
  61.1 4.7 copy.82
  69.4 0.6 fusion.18
  70.0 8.9 bitcast_multiply_fusion.2
  78.9 4.2 bitcast_multiply_fusion.1
  83.1 4.2 bitcast_multiply_fusion
  87.3 306.5 %all-gather.2.cloned.1.call-done = bf16[4096,128]{1,0:T(8,128)(2,1)} async-done(((bf16[16,128]{1,0:T(8,128)(2,1)}), bf16[4096,128]{1,0:T(8,128)(2,1)}) %all-gather.2.cloned.1.call-update) | async-done | bytes 1048592 | tf_op jit(solution)/shard_map/all_gather | solution.py:69
  393.8 1.5 copy.53
  395.4 0.1 fusion.34
  395.4 0.1 copy.68
  395.6 0.1 copy.69
  395.7 0.1 copy.74
  395.8 0.1 copy.75
  395.9 0.1 fusion.32
  396.0 0.1 copy.70
  396.1 0.1 copy.71
  396.2 0.1 copy.76
  396.3 0.1 copy.77
  396.4 0.1 fusion.30
  396.5 0.1 copy.72
  396.6 0.1 copy.73
  396.7 0.1 copy.78
  396.8 0.1 copy.79
  397.0 8.5 add_reduce_fusion.2
  405.5 0.2 broadcast.110.clone.1
  405.8 5.2 add_reduce_fusion.1
  411.0 5.2 add_reduce_fusion
  416.2 0.2 broadcast.110.clone
  416.6 0.3 add.106
  416.8 1.9 copy.66
  418.7 3.1 copy.67
  421.8 0.0 reduce-scatter.2.cloned.1.call-update
  421.8 1285.6 %reduce-scatter.2.cloned.1.call-done = f32[16,128]{1,0:T(8,128)} async-done(((f32[4096,128]{1,0:T(8,128)}), f32[16,128]{1,0:T(8,128)}) %reduce-scatter.2.cloned.1.call-update) | async-done | bytes 8208 | tf_op jit(solution)/shard_map/reduce_scatter | solution.py:96
  (40 shorter events, 0.2 us)
Async XLA Ops:
  6.5 387.3 %all-gather.2.cloned.1.call-start = ((), (), s32[]{:S(2)}) async-start(), calls=%async_computation.1 | async-start | bytes 1052672 | tf_op jit(solution)/shard_map/all_gather | solution.py:69
  7.3 1700.2 %reduce-scatter.2.cloned.1.call-start = ((), (), s32[]{:S(2)}) async-start(), calls=%async_computation.2 | async-start | bytes 2105344 | tf_op jit(solution)/shard_map/reduce_scatter | solution.py:96
  44.6 16.4 slice-start.4
  52.9 8.2 slice-start.5
  70.0 8.9 copy-start.1
  70.0 13.1 slice-start.2
  78.9 4.2 slice-start.3
  396.9 8.8 copy-start
  397.0 14.0 slice-start
  405.5 5.5 slice-start.1
Sparse Core Ops, SparseCore 0:
  9.1 384.6 all-gather.1
  421.9 1285.4 reduce-scatter.1
where the time goes:
time: 1710 us
  waiting for transfers between devices  1590 us (93%)
  other arithmetic  40.8 us (2%)
  local copies, waits for them, and re-layouts  38.9 us (2%)
  between operations  28.2 us (2%)
    reduce_scatter x1, waiting for transfers between devices, on_device(): lax.psum_scatter(gradient, ('row', 'col'), scatter_dimension=0, tiled=True)  1290 us
    all_gather x1, waiting for transfers between devices, on_device(): gathered = lax.all_gather(spectra, ('row', 'col'), axis=0, tiled=True)  307 us
  transfers between devices with their start and end apart: 2, of which 2 were waited for; matrix products, arithmetic and copies ran while one was open for 4% of the time, Pallas kernels for 0%

commit v1 on v0

--- a/solution.py
+++ b/solution.py
@@ -1,8 +1,20 @@
+import functools
 import math
 import jax
 import jax.numpy as jnp
 from jax import lax
 from jax.sharding import PartitionSpec as P
+
+
+def group_spread(incoming_x, shard_axis):
+    r_now = lax.axis_size(shard_axis)
+    block_now = jnp.stack(r_now * [incoming_x], 0)
+    then = lax.all_to_all(block_now, axis_name=shard_axis, split_axis=0, concat_axis=0)
+    w2 = jnp.concatenate(then, axis=0)
+    return w2
+
+
+review_sheet = functools.partial(group_spread, shard_axis=("row", "col"))
 
 
 def dft_table(lag_count, freq_count):
@@ -66,7 +78,7 @@
     filled = slot_tile >= 0
     station_ids = jnp.arange(tile_size, dtype=jnp.int32)
     upper = station_ids[:, None] < station_ids[None, :]
-    gathered = lax.all_gather(spectra, ("row", "col"), axis=0, tiled=True)
+    gathered = review_sheet(spectra)
     row_source = block_major(gathered, row_count, col_count, block_count, tile_size)
     row_div = 1
     col_div = 1

time: 1710 us -> 1430 us (0.84)
  waiting for transfers between devices: 1590 us -> 1290 us
    all_gather x1 -> x0, waiting for transfers between devices: 307 us -> none  [on_device(): gathered = lax.all_gather(spectra, ('row', 'col'), axis=0, tiled=True)]
  transfers between devices with their start and end apart: 2 -> 2, of which waited for: 2 -> 1; matrix products, arithmetic and copies ran while one was open for 4% -> 5% of each run, Pallas kernels for 0% -> 0%
where the time goes in v1:
time: 1430 us
  waiting for transfers between devices  1290 us (90%)
  other arithmetic  40.9 us (3%)
  local copies, waits for them, and re-layouts  39.6 us (3%)
  between operations  28.2 us (2%)
  starting transfers between devices  14.6 us (1%)
    reduce_scatter x1, waiting for transfers between devices, on_device(): lax.psum_scatter(gradient, ('row', 'col'), scatter_dimension=0, tiled=True)  1290 us
  transfers between devices with their start and end apart: 2, of which 1 were waited for; matrix products, arithmetic and copies ran while one was open for 5% of the time, Pallas kernels for 0%

profile of v1, /device:TPU:0, one launch (start us, length us, event | category | flops | bytes accessed | tf_op | source)
XLA Modules:
  0.0 1428.7 jit_solution(10225532969479599324)
XLA Ops:
  6.5 1.8 stack.2
  8.3 14.6 %all-to-all-start = ((bf16[256,16,128]{2,1,0:T(8,128)(2,1)}), bf16[256,16,128]{2,1,0:T(8,128)(2,1)S(1)}, u32[]{:S(2)}, u32[]{:S(2)}) async-start(bf16[256,16,128]{2,1,0:T(8,128)(2,1)} %stack.2), calls=%async_computation | async-start | bytes 2097152 | tf_op jit(solution)/shard_map/all_to_all | solution.py:12
  22.9 0.0 reduce-scatter.2.cloned.1.call-start
  23.0 0.7 fusion.25
  23.7 0.7 broadcast_compare_fusion
  24.4 0.8 multiply_reduce_fusion
  25.2 0.6 fusion.36
  25.8 0.7 fusion.37
  26.5 0.2 multiply_convert_fusion.1
  26.6 8.4 fusion.29
  35.0 4.5 convolution_bitcast_fusion.2
  39.5 4.5 convolution_bitcast_fusion.1
  43.9 4.5 convolution_bitcast_fusion
  49.5 0.6 fusion.14
  51.3 0.7 fusion.16
  60.5 8.2 copy.81
  68.7 8.2 copy.82
  76.9 4.7 copy.83
  85.2 0.6 fusion.18
  85.9 8.9 bitcast_multiply_fusion.2
  94.8 4.2 bitcast_multiply_fusion.1
  99.0 4.2 bitcast_multiply_fusion
  103.1 0.3 copy.54
  103.5 0.1 fusion.34
  103.5 0.1 copy.69
  103.7 0.1 copy.70
  103.8 0.1 copy.75
  103.9 0.1 copy.76
  104.0 0.1 fusion.32
  104.1 0.1 copy.71
  104.2 0.1 copy.72
  104.3 0.1 copy.77
  104.4 0.1 copy.78
  104.5 0.1 fusion.30
  104.6 0.1 copy.73
  104.7 0.1 copy.74
  104.8 0.1 copy.79
  104.9 0.1 copy.80
  105.1 8.6 add_reduce_fusion.2
  113.7 0.2 broadcast.112.clone.1
  113.9 5.2 add_reduce_fusion.1
  119.2 5.2 add_reduce_fusion
  124.4 0.2 broadcast.112.clone
  124.7 0.3 add.106
  124.9 1.9 copy.67
  126.8 3.1 copy.68
  129.9 0.0 reduce-scatter.2.cloned.1.call-update
  129.9 1291.9 %reduce-scatter.2.cloned.1.call-done = f32[16,128]{1,0:T(8,128)} async-done(((f32[4096,128]{1,0:T(8,128)}), f32[16,128]{1,0:T(8,128)}) %reduce-scatter.2.cloned.1.call-update) | async-done | bytes 8208 | tf_op jit(solution)/shard_map/reduce_scatter | solution.py:108
  (40 shorter events, 0.2 us)
Async XLA Ops:
  8.3 94.8 %all-to-all-start = ((bf16[256,16,128]{2,1,0:T(8,128)(2,1)}), bf16[256,16,128]{2,1,0:T(8,128)(2,1)S(1)}, u32[]{:S(2)}, u32[]{:S(2)}) async-start(bf16[256,16,128]{2,1,0:T(8,128)(2,1)} %stack.2), calls=%async_computation | async-start | bytes 2097152 | tf_op jit(solution)/shard_map/all_to_all | solution.py:12
  22.9 1398.9 %reduce-scatter.2.cloned.1.call-start = ((), (), s32[]{:S(2)}) async-start(), calls=%async_computation.2 | async-start | bytes 2105344 | tf_op jit(solution)/shard_map/reduce_scatter | solution.py:108
  60.5 16.4 %slice-start.4 = ((s8[8388608]{0:T(1024)(128)(4,1)}), s8[4194304]{0:T(1024)(128)(4,1)S(1)}, s32[]{:S(2)}) async-start(s8[8388608]{0:T(1024)(128)(4,1)} %bitcast.92), calls=%async_computation.7 | async-start | bytes 8388608
  68.7 8.2 slice-start.5
  85.9 8.9 copy-start.1
  85.9 13.1 slice-start.2
  94.8 4.2 slice-start.3
  105.0 8.9 copy-start
  105.1 14.1 slice-start
  113.7 5.5 slice-start.1
Sparse Core Ops, SparseCore 0:
  130.0 1291.7 reduce-scatter.1
